TPU v7x, 768 devices: a whole 4x8x12 slice. The times are simulated.
768 devices in a mesh: ta: 128 (over z_lo, y, x), gz: 6 (over z_hi, core).
Axes of the slice: x: 4, y: 8, z: 12 (z_hi: 3, z_lo: 4; z = z_hi * 4 + z_lo), core: 2. Of those that a mesh axis runs over, the one named last changes fastest.
Arguments:
- links: float32 [4, 2, 3, 3, 128, 12, 128], P(None, None, None, None, 'ta', 'gz'), may hold values from -1 to 1, as said below
Outputs:
- flowed: float32 [4, 2, 3, 3, 128, 12, 128], P(None, None, None, None, 'ta', 'gz')
- loops: float32 [2, 3, 3, 128, 12, 128], P(None, None, None, 'ta', 'gz')
Inputs may be any that keep to these rules, and one draw needn't show every extreme that they name: `links`: every link is a special unitary 3x3 matrix, given by its real and imaginary parts.
All inputs are finite; a program needn't handle non-finite values.
Results may differ from a plain program's by a relative error of at most 0.0001.
Values sent between devices are 32-bit elements; how exact they have to be, the bound alone decides.
A program may use at most 32 MiB of HBM per device.

v0:
```python
import jax
import jax.numpy as jnp
from jax import lax
from jax.sharding import PartitionSpec as P

LX = 8
LY = 16


def padded_2(cells, sides, width):
    for axis, dim in sides:
        count = lax.axis_size(axis)
        head = lax.slice_in_dim(cells, 0, width, axis=dim)
        tail = lax.slice_in_dim(cells, cells.shape[dim] - width, cells.shape[dim], axis=dim)
        cells = jnp.concatenate(
            [
                lax.ppermute(tail, axis, [(i, (i + 1) % count) for i in range(count)]),
                cells,
                lax.ppermute(head, axis, [((i + 1) % count, i) for i in range(count)]),
            ],
            axis=dim,
        )
    return cells


def passed_along(value, axis, steps):
    count = lax.axis_size(axis)
    pairs = [(source, (source + steps) % count) for source in range(count)]
    return lax.ppermute(value, axis, pairs)


def real_product(left, right):
    return jnp.sum(left[:, :, None] * right[None, :, :], axis=1)


def product(left, right):
    real_part = real_product(left[0], right[0]) - real_product(left[1], right[1])
    imag_part = real_product(left[0], right[1]) + real_product(left[1], right[0])
    return jnp.stack([real_part, imag_part])


def adjoint(matrix):
    return jnp.stack([jnp.swapaxes(matrix[0], 0, 1), -jnp.swapaxes(matrix[1], 0, 1)])


def identity_like(matrix):
    tail = matrix.shape[3:]
    eye_part = jnp.broadcast_to(
        jnp.eye(3, dtype=jnp.float32).reshape((3, 3) + (1,) * len(tail)), (3, 3) + tail
    )
    return jnp.stack([eye_part, jnp.zeros((3, 3) + tail, jnp.float32)])


def shifted(padded, direction, offset):
    field = padded[direction]
    steps = field.shape[-3] - 2
    depth = field.shape[-2] - 2
    core = field[
        ..., 1 + offset[0] : 1 + offset[0] + steps, 1 + offset[1] : 1 + offset[1] + depth, :
    ]
    if offset[2] != 0 or offset[3] != 0:
        grid = core.reshape(core.shape[:-1] + (LX, LY))
        grid = jnp.roll(grid, (-offset[2], -offset[3]), axis=(-2, -1))
        core = grid.reshape(core.shape)
    return core


def unit_step(direction):
    table = ((1, 0, 0, 0), (0, 0, 1, 0), (0, 0, 0, 1), (0, 1, 0, 0))
    return table[direction]


def traceless_part(omega):
    real_part = 0.5 * (omega[0] - jnp.swapaxes(omega[0], 0, 1))
    imag_part = 0.5 * (omega[1] + jnp.swapaxes(omega[1], 0, 1))
    trace_imag = (imag_part[0, 0] + imag_part[1, 1] + imag_part[2, 2]) / 3.0
    eye_part = jnp.eye(3, dtype=jnp.float32).reshape((3, 3) + (1,) * trace_imag.ndim)
    imag_part = imag_part - eye_part * trace_imag[None, None]
    return jnp.stack([real_part, imag_part])


def flow_links(padded):
    zero = (0, 0, 0, 0)
    results = []
    for direction in range(4):
        link = shifted(padded, direction, zero)
        step_main = unit_step(direction)
        total = jnp.zeros_like(link)
        for other in range(4):
            if other == direction:
                continue
            step_other = unit_step(other)
            minus_other = tuple((-value for value in step_other))
            cross = tuple((a - b for a, b in zip(step_main, step_other)))
            upper = product(
                product(
                    shifted(padded, other, step_main),
                    adjoint(shifted(padded, direction, step_other)),
                ),
                adjoint(shifted(padded, other, zero)),
            )
            lower = product(
                product(
                    adjoint(shifted(padded, other, cross)),
                    adjoint(shifted(padded, direction, minus_other)),
                ),
                shifted(padded, other, minus_other),
            )
            total = total + upper + lower
        omega = product(link, total)
        generator = -0.25 * traceless_part(omega)
        unity = identity_like(link)
        series = unity
        for order in range(6, 0, -1):
            series = unity + product(generator, series) / float(order)
        results.append(product(series, link))
    return jnp.stack(results)


def local_chain(lines):
    count = lines.shape[3]
    slices = [lines[:, :, :, 0]]
    unity = identity_like(slices[0])
    prefixes = [unity]
    index = 0
    prefixes.append(product(prefixes[-1], slices[index]))
    suffixes = [unity] * count
    suffix = unity
    index = 0
    suffix = product(slices[index], suffix)
    suffixes[index] = suffix
    return (prefixes[count], prefixes, suffixes)


def local(links):
    padded = padded_2(links, (("ta", 4), ("gz", 5)), 1)
    flowed = flow_links(padded)
    total, prefixes, suffixes = local_chain(flowed[0])
    unity = identity_like(total)

    def advance(index, carry):
        message, gathered = carry
        message = passed_along(message, "ta", -1)
        return (message, product(gathered, message))

    carried, others = lax.fori_loop(0, lax.axis_size("ta") - 1, advance, (total, unity))
    loops = jnp.stack([product(product(suffixes[0], others), prefixes[0])], axis=3)
    return (flowed, loops)


def solution(mesh):
    placed = (P(None, None, None, None, "ta", "gz", None),)
    return jax.shard_map(
        local,
        mesh=mesh,
        in_specs=placed,
        out_specs=(
            P(None, None, None, None, "ta", "gz", None),
            P(None, None, None, "ta", "gz", None),
        ),
        check_vma=False,
    )
```

profile of v0, /device:TPU:254, one launch (start us, length us, event | category | flops | bytes accessed | tf_op | source)
XLA Modules:
  0.0 1614.8 jit_solution(4209485877026776841)
XLA Ops:
  113.7 1499.2 %while.12 = (s32[]{:T(128)}, f32[2,3,3,2,128]{4,3,2,1,0:T(2,128)S(1)}, f32[2,3,3,2,128]{4,3,2,1,0:T(2,128)S(1)}, s32[]{:T(128)}) while((s32[]{:T(128)}, f32[2,3,3,2,128]{4,3,2,1,0:T(2,128)S(1)}, f32[2,3,3,2,128]{4,3,2,1,0:T(2,128)S(1)}, s32[]{:T(128)}) %tuple.461), condition=%wide.region_331.332_spmd, body=%wide.region_326.331_spmd.sunk | while | flops 55298 | bytes 350301 | solution.py:146
  127.5 9.7 collective-permute-done
  162.9 9.7 collective-permute-done
  198.3 9.7 collective-permute-done
  233.7 9.7 collective-permute-done
  245.5 9.7 collective-permute-done
  269.1 9.8 collective-permute-done
  292.7 9.7 collective-permute-done
  328.1 9.7 collective-permute-done
  363.5 9.7 collective-permute-done
  375.3 9.7 collective-permute-done
  410.7 9.7 collective-permute-done
  446.1 9.7 collective-permute-done
  481.5 9.7 collective-permute-done
  516.9 9.7 collective-permute-done
  552.3 9.7 collective-permute-done
  587.7 9.7 collective-permute-done
  599.5 9.8 collective-permute-done
  623.2 9.7 collective-permute-done
  658.6 9.7 collective-permute-done
  694.0 9.7 collective-permute-done
  705.8 9.7 collective-permute-done
  741.2 9.7 collective-permute-done
  776.6 9.7 collective-permute-done
  812.0 9.7 collective-permute-done
  847.4 9.7 collective-permute-done
  882.8 9.7 collective-permute-done
  918.2 9.7 collective-permute-done
  930.0 9.9 collective-permute-done
  942.0 9.7 collective-permute-done
  977.4 9.7 collective-permute-done
  1012.8 9.7 collective-permute-done
  1024.6 9.7 collective-permute-done
  1048.2 9.7 collective-permute-done
  1071.8 9.7 collective-permute-done
  1107.2 9.7 collective-permute-done
  1119.0 9.7 collective-permute-done
  1154.4 9.7 collective-permute-done
  1189.8 9.7 collective-permute-done
  1225.2 9.7 collective-permute-done
  1260.6 9.9 collective-permute-done
  1284.4 9.7 collective-permute-done
  1296.2 9.7 collective-permute-done
  1331.6 9.7 collective-permute-done
  1367.0 9.7 collective-permute-done
  1402.4 9.7 collective-permute-done
  1437.8 9.7 collective-permute-done
  1473.2 9.7 collective-permute-done
  (1657 shorter events, 1145.8 us)
Async XLA Ops:
  8.5 12.5 collective-permute-start.2
  113.7 11.7 collective-permute-start
  125.5 11.7 collective-permute-start
  137.3 11.7 collective-permute-start
  149.1 11.7 collective-permute-start
  160.9 11.7 collective-permute-start
  172.7 11.7 collective-permute-start
  184.5 11.7 collective-permute-start
  196.3 11.7 collective-permute-start
  208.1 11.7 collective-permute-start
  219.9 11.7 collective-permute-start
  231.7 11.7 collective-permute-start
  243.5 11.7 collective-permute-start
  255.3 11.7 collective-permute-start
  267.1 11.7 collective-permute-start
  279.0 11.7 collective-permute-start
  290.8 11.7 collective-permute-start
  302.6 11.7 collective-permute-start
  314.4 11.7 collective-permute-start
  326.2 11.7 collective-permute-start
  338.0 11.7 collective-permute-start
  349.8 11.7 collective-permute-start
  361.6 11.7 collective-permute-start
  373.4 11.7 collective-permute-start
  385.2 11.7 collective-permute-start
  408.8 11.7 collective-permute-start
  420.6 11.7 collective-permute-start
  432.4 11.7 collective-permute-start
  444.2 11.7 collective-permute-start
  456.0 11.7 collective-permute-start
  467.8 11.7 collective-permute-start
  479.6 11.7 collective-permute-start
  491.4 11.7 collective-permute-start
  503.2 11.7 collective-permute-start
  515.0 11.7 collective-permute-start
  526.8 11.7 collective-permute-start
  538.6 11.7 collective-permute-start
  550.4 11.7 collective-permute-start
  562.2 11.7 collective-permute-start
  574.0 11.7 collective-permute-start
  585.8 11.7 collective-permute-start
  597.6 11.8 collective-permute-start
  609.5 11.7 collective-permute-start
  621.3 11.7 collective-permute-start
  633.1 11.7 collective-permute-start
  928.1 11.8 collective-permute-start
  1046.2 11.7 collective-permute-start
  1258.7 11.9 collective-permute-start
  (178 other events, 1036.2 us)
where the time goes:
time: 1620 us; the launch traced here: 1610 us
  waiting for transfers between devices  1250 us (77%)
  starting transfers between devices  263 us (16%)
  local copies, waits for them, and re-layouts  60.8 us (4%)
  other arithmetic  30.2 us (2%)
    ppermute x127, waiting for transfers between devices, passed_along(): return lax.ppermute(value, axis, pairs)  1240 us
    ppermute x127, starting transfers between devices, passed_along(): return lax.ppermute(value, axis, pairs)  244 us
    unnamed x192, local copies, waits for them, and re-layouts  33.8 us
  transfers between devices with their start and end apart: 131, of which 131 were waited for; matrix products, arithmetic and copies ran while one was open for 0% of the time, Pallas kernels for 0%

commit v1 on v0

v1 whole, which is shorter than its diff:
```python
import jax
import jax.numpy as jnp
from jax import lax
from jax.experimental import pallas as pl
from jax.experimental.pallas import tpu as pltpu
from jax.sharding import PartitionSpec as P

LX = 8
LY = 16
LANES = LX * LY
MESH = pl.DeviceIdType.MESH


def factors(count):
    first = 4 if count % 4 == 0 and count > 8 else 2
    rest = count // first
    third = 4 if rest % 4 == 0 and rest > 4 else 2
    return first, rest // third, third


def greet(peers):
    barrier = pltpu.get_barrier_semaphore()
    for peer in peers:
        pl.semaphore_signal(barrier, inc=1, device_id=peer, device_id_type=MESH)
    pl.semaphore_wait(barrier, len(peers))


def halo_kernel(count_t, count_z, u, tp, tm, zp, zm, cz, ct, send, recv):
    t = lax.axis_index("ta")
    z = lax.axis_index("gz")
    t_next, t_prev = lax.rem(t + 1, count_t), lax.rem(t + count_t - 1, count_t)
    z_next, z_prev = lax.rem(z + 1, count_z), lax.rem(z + count_z - 1, count_z)
    plan = [
        (u.at[pl.ds(3, 1)], cz, (t_prev, z_next)),
        (u.at[pl.ds(0, 1)], ct, (t_next, z_prev)),
        (u, zm, (t, z_next)),
        (u.at[pl.ds(0, 3)], zp, (t, z_prev)),
        (u, tm, (t_next, z)),
        (u.at[pl.ds(1, 3)], tp, (t_prev, z)),
    ]
    greet([peer for _, _, peer in plan])
    copies = [
        pltpu.make_async_remote_copy(
            src_ref=source,
            dst_ref=target,
            send_sem=send.at[index],
            recv_sem=recv.at[index],
            device_id=peer,
            device_id_type=MESH,
        )
        for index, (source, target, peer) in enumerate(plan)
    ]
    for copy in copies:
        copy.start()
    for copy in copies:
        copy.wait()


def halos(links, count_t, count_z):
    tail = links.shape[1:]
    shapes = [(n,) + tail for n in (3, 4, 3, 4, 1, 1)]
    return pl.pallas_call(
        lambda *refs: halo_kernel(count_t, count_z, *refs),
        out_shape=[jax.ShapeDtypeStruct(shape, jnp.float32) for shape in shapes],
        in_specs=[pl.BlockSpec(memory_space=pl.ANY)],
        out_specs=[pl.BlockSpec(memory_space=pl.ANY)] * 6,
        scratch_shapes=[pltpu.SemaphoreType.DMA((6,)), pltpu.SemaphoreType.DMA((6,))],
        compiler_params=pltpu.CompilerParams(collective_id=0, has_side_effects=True),
        name="halo_exchange",
    )(links)


def entry(matrix, row, col, adjoint):
    if adjoint:
        return matrix[col * 3 + row], matrix[9 + col * 3 + row], -1
    return matrix[row * 3 + col], matrix[9 + row * 3 + col], 1


def tile_product(left, right, left_adjoint=False, right_adjoint=False):
    real, imag = [], []
    for row in range(3):
        for col in range(3):
            re = im = None
            for mid in range(3):
                a, b, s = entry(left, row, mid, left_adjoint)
                c, d, r = entry(right, mid, col, right_adjoint)
                ac, bd, ad, bc = a * c, b * d, a * d, b * c
                re_term = ac - bd if s * r > 0 else ac + bd
                re = re_term if re is None else re + re_term
                if im is None:
                    if r > 0:
                        im = ad + bc if s > 0 else ad - bc
                    else:
                        im = bc - ad if s > 0 else -(ad + bc)
                else:
                    im = im + ad if r > 0 else im - ad
                    im = im + bc if s > 0 else im - bc
            real.append(re)
            imag.append(im)
    return real + imag


def flow_kernel(u, tp, tm, zp, zm, cz, ct, flowed, line, pk, fields):
    for i in range(18):
        for mu in range(4):
            rows = slice(2 * mu, 2 * mu + 2)
            pk[0, i, rows, :] = u[mu, i]
            pk[2, i, rows, :] = tm[mu, i]
            pk[4, i, 2 * mu : 2 * mu + 1, :] = zm[mu, i, 1:2]
            pk[4, i, 2 * mu + 1 : 2 * mu + 2, :] = u[mu, i, 0:1]
            if mu > 0:
                pk[1, i, rows, :] = tp[mu - 1, i]
            if mu < 3:
                pk[3, i, 2 * mu : 2 * mu + 1, :] = u[mu, i, 1:2]
                pk[3, i, 2 * mu + 1 : 2 * mu + 2, :] = zp[mu, i, 0:1]
        pk[5, i, 0:1, :] = tm[0, i, 1:2]
        pk[5, i, 1:2, :] = ct[0, i, 0:1]
        pk[5, i, 6:7, :] = cz[0, i, 1:2]
        pk[5, i, 7:8, :] = tp[2, i, 0:1]
    group = lax.broadcasted_iota(jnp.int32, (8, LANES), 0) // 2
    y = lax.broadcasted_iota(jnp.int32, (8, LANES), 1) % LY

    def pick(tiles):
        rest = jnp.where(group == 2, tiles[2], tiles[3])
        return jnp.where(group == 0, tiles[0], jnp.where(group == 1, tiles[1], rest))

    def x_plus(tile):
        return pltpu.roll(tile, LANES - LY, 1)

    def x_minus(tile):
        return pltpu.roll(tile, LY, 1)

    def y_plus(tile):
        return jnp.where(
            y == LY - 1, pltpu.roll(tile, LY - 1, 1), pltpu.roll(tile, LANES - 1, 1)
        )

    def y_minus(tile):
        return jnp.where(
            y == 0, pltpu.roll(tile, LANES - LY + 1, 1), pltpu.roll(tile, 1, 1)
        )

    def lowered(tile, k):
        return pltpu.roll(tile, 8 - 2 * k, 0)

    for i in range(18):
        here, t_up, t_down, z_up, z_down, corner = (pk[f, i] for f in range(6))
        up = [t_up, x_plus(here), y_plus(here), z_up]
        down = [t_down, x_minus(here), y_minus(here), z_down]
        base = pick(down)
        t_side = [None, corner, y_plus(t_down), x_plus(t_down)]
        z_side = [None, y_plus(z_down), x_plus(z_down), corner]
        for k in range(1, 4):
            ahead = pick([up[(nu - k) % 4] for nu in range(4)])
            behind = pick([down[(nu - k) % 4] for nu in range(4)])
            cross = pick([t_side[k], x_minus(ahead), y_minus(ahead), z_side[k]])
            fields[0, k - 1, i] = lowered(ahead, k)
            fields[1, 3 - k, i] = ahead
            fields[2, k - 1, i] = lowered(here, k)
            fields[3, k - 1, i] = lowered(cross, k)
            fields[4, 3 - k, i] = behind
            fields[5, k - 1, i] = lowered(base, k)

    def load(field, k):
        return [fields[field, k, i] for i in range(18)]

    total = None
    for k in range(3):
        upper = tile_product(load(0, k), load(1, k), False, True)
        upper = tile_product(upper, load(2, k), False, True)
        lower = tile_product(load(3, k), load(4, k), True, True)
        lower = tile_product(lower, load(5, k))
        both = [a + b for a, b in zip(upper, lower)]
        total = both if total is None else [a + b for a, b in zip(total, both)]
    link = [pk[0, i] for i in range(18)]
    omega = tile_product(link, total)
    trace = (omega[9] + omega[13] + omega[17]) * (1.0 / 3.0)
    generator = [None] * 18
    for row in range(3):
        for col in range(3):
            a, b = row * 3 + col, col * 3 + row
            generator[a] = -0.125 * (omega[a] - omega[b])
            part = 0.5 * (omega[9 + a] + omega[9 + b])
            if row == col:
                part = part - trace
            generator[9 + a] = -0.25 * part

    def plus_unity(matrix):
        return [v + 1.0 if i in (0, 4, 8) else v for i, v in enumerate(matrix)]

    series = plus_unity([v * (1.0 / 6.0) for v in generator])
    for order in range(5, 0, -1):
        series = tile_product(generator, series)
        series = plus_unity([v * (1.0 / order) for v in series])
    result = tile_product(series, link)
    for i in range(18):
        for mu in range(4):
            flowed[mu, i] = result[i][2 * mu : 2 * mu + 2]
        line[i] = result[i][0:2]


def flow(links, around):
    vmem = pl.BlockSpec(memory_space=pltpu.VMEM)
    return pl.pallas_call(
        flow_kernel,
        out_shape=[
            jax.ShapeDtypeStruct(links.shape, jnp.float32),
            jax.ShapeDtypeStruct(links.shape[1:], jnp.float32),
        ],
        in_specs=[vmem] * 7,
        out_specs=[vmem] * 2,
        scratch_shapes=[
            pltpu.VMEM((6, 18, 8, LANES), jnp.float32),
            pltpu.VMEM((6, 3, 18, 8, LANES), jnp.float32),
        ],
        name="flow_links",
    )(links, *around)


def product(left, right):
    re = im = None
    for mid in range(3):
        a, b = left[0][:, mid : mid + 1], left[1][:, mid : mid + 1]
        c, d = right[0][mid : mid + 1], right[1][mid : mid + 1]
        re_term, im_term = a * c - b * d, a * d + b * c
        re = re_term if re is None else re + re_term
        im = im_term if im is None else im + im_term
    return re, im


def loops_kernel(count, line, out, slots1, slots2, slots3, row_total, plane_total, send, recv):
    sizes = factors(count)
    t = lax.axis_index("ta")
    z = lax.axis_index("gz")
    strides = (1, sizes[0], sizes[0] * sizes[1])
    digits = [lax.rem(t // stride, size) for stride, size in zip(strides, sizes)]
    slots = (slots1, slots2, slots3)

    def peer(stage, offset):
        size, stride, digit = sizes[stage], strides[stage], digits[stage]
        moved = lax.rem(digit + size - offset, size)
        return (t + (moved - digit) * stride, z)

    greet([peer(s, d) for s in range(3) for d in range(1, sizes[s])])
    shape = (3, 3) + line.shape[-2:]
    diagonal = [
        [jnp.full(shape[2:], 1.0 if a == b else 0.0, jnp.float32) for b in range(3)]
        for a in range(3)
    ]
    unity = jnp.stack([jnp.stack(row) for row in diagonal])
    nought = jnp.zeros(shape, jnp.float32)
    start = [0, sizes[0] - 1, sizes[0] + sizes[1] - 2]

    def share(stage, source):
        copies = []
        for offset in range(1, sizes[stage]):
            index = start[stage] + offset - 1
            copies.append(
                pltpu.make_async_remote_copy(
                    src_ref=source,
                    dst_ref=slots[stage].at[offset - 1],
                    send_sem=send.at[index],
                    recv_sem=recv.at[index],
                    device_id=peer(stage, offset),
                    device_id_type=MESH,
                )
            )
        for copy in copies:
            copy.start()
        return copies

    def ordered(stage, copies):
        after = before = None
        for offset in range(1, sizes[stage]):
            copies[offset - 1].wait_recv()
            re, im = slots[stage][offset - 1, 0], slots[stage][offset - 1, 1]
            inside = digits[stage] + offset < sizes[stage]
            high = (jnp.where(inside, re, unity), jnp.where(inside, im, nought))
            low = (jnp.where(inside, unity, re), jnp.where(inside, nought, im))
            after = high if after is None else product(after, high)
            before = low if before is None else product(before, low)
        return after, before

    copies1 = share(0, line)
    row_after, row_before = ordered(0, copies1)
    row_after = product((line[0], line[1]), row_after)
    row = product(row_before, row_after)
    row_total[0], row_total[1] = row
    copies2 = share(1, row_total)
    plane_after, plane_before = ordered(1, copies2)
    plane = product(plane_before, product(row, plane_after))
    plane_total[0], plane_total[1] = plane
    copies3 = share(2, plane_total)
    left = product(row_after, plane_after)
    right = product(plane_before, row_before)
    for offset in range(1, sizes[2]):
        copies3[offset - 1].wait_recv()
        left = product(left, (slots3[offset - 1, 0], slots3[offset - 1, 1]))
    result = product(left, right)
    out[0], out[1] = result
    for copy in copies1 + copies2 + copies3:
        copy.wait_send()


def loops_of(line, count):
    sizes = factors(count)
    vmem = pl.BlockSpec(memory_space=pltpu.VMEM)
    messages = sum(sizes) - 3
    return pl.pallas_call(
        lambda *refs: loops_kernel(count, *refs),
        out_shape=jax.ShapeDtypeStruct(line.shape, jnp.float32),
        in_specs=[vmem],
        out_specs=vmem,
        scratch_shapes=[
            pltpu.VMEM((sizes[0] - 1,) + line.shape, jnp.float32),
            pltpu.VMEM((sizes[1] - 1,) + line.shape, jnp.float32),
            pltpu.VMEM((sizes[2] - 1,) + line.shape, jnp.float32),
            pltpu.VMEM(line.shape, jnp.float32),
            pltpu.VMEM(line.shape, jnp.float32),
            pltpu.SemaphoreType.DMA((messages,)),
            pltpu.SemaphoreType.DMA((messages,)),
        ],
        compiler_params=pltpu.CompilerParams(collective_id=1, has_side_effects=True),
        name="temporal_loops",
    )(line)


def local(links):
    count_t, count_z = lax.axis_size("ta"), lax.axis_size("gz")
    packed = links.reshape(4, 18, 2, LANES)
    flowed, line = flow(packed, halos(packed, count_t, count_z))
    loops = loops_of(line.reshape(2, 3, 3, 2, LANES), count_t)
    return flowed.reshape(links.shape), loops.reshape(2, 3, 3, 1, 2, LANES)


def solution(mesh):
    return jax.shard_map(
        local,
        mesh=mesh,
        in_specs=(P(None, None, None, None, "ta", "gz", None),),
        out_specs=(
            P(None, None, None, None, "ta", "gz", None),
            P(None, None, None, "ta", "gz", None),
        ),
        check_vma=False,
    )
```

time: 1620 us -> 50.5 us (0.03)
  the two profiles are of different devices: /device:TPU:254 before, /device:TPU:2 now
where the time goes in v1:
time: 50.5 us; the launch traced here: 50.1 us
  Pallas kernels  48.2 us (95%)
  local copies, waits for them, and re-layouts  1.33 us (3%)
  between operations  0.65 us (1%)
    pallas_call x1, Pallas kernels, loops_of(): pl.pallas_call(lambda *refs: loops_kernel(count, *refs), out_shape=jax.Sh...  23.2 us
    pallas_call x1, Pallas kernels, halos(): pl.pallas_call(lambda *refs: halo_kernel(count_t, count_z, *refs), out_sh...  21.8 us
    pallas_call x1, Pallas kernels, flow(): pl.pallas_call(flow_kernel, out_shape=[jax.ShapeDtypeStruct(links.shape,...  3.13 us
    unnamed x1, local copies, waits for them, and re-layouts  1.33 us

profile of v1, /device:TPU:2, one launch (start us, length us, event | category | flops | bytes accessed | tf_op | source)
XLA Modules:
  0.0 50.1 jit_solution(1045396744199771140)
XLA Ops:
  0.6 21.8 %halo_exchange.1 = (f32[3,18,2,128]{3,2,1,0:T(2,128)}, f32[4,18,2,128]{3,2,1,0:T(2,128)}, f32[3,18,2,128]{3,2,1,0:T(2,128)}, f32[4,18,2,128]{3,2,1,0:T(2,128)}, ...) custom-call(f32[4,18,2,128]{3,2,1,0:T(2,128)} %bitcast.8), custom_call_target="tpu_custom_call" | custom-call | tf_op jit(solution)/shard_map/halo_exchange/pallas_call | solution.py:62
  22.5 3.1 %flow_links.1 = (f32[4,18,2,128]{3,2,1,0:T(2,128)}, f32[18,2,128]{2,1,0:T(2,128)}) custom-call(f32[4,18,2,128]{3,2,1,0:T(2,128)} %bitcast.9, f32[3,18,2,128]{3,2,1,0:T(2,128)} %get-tuple-element.10.tp, f32[4,18,2,128]{3,2,1,0:T(2,128)} %get-tuple-element.11.tm, f32[3,18,2,128]{3,2,1,0:T(2,128)} %get-tuple-element.12.zp, ...), custom_call_target="tpu_custom_call" | custom-call | tf_op jit(solution)/shard_map/flow_links/pallas_call | solution.py:204
  25.6 23.2 %temporal_loops.1 = f32[2,3,3,2,128]{4,3,2,1,0:T(2,128)} custom-call(f32[2,3,3,2,128]{4,3,2,1,0:T(2,128)} %bitcast.11), custom_call_target="tpu_custom_call" | custom-call | tf_op jit(solution)/shard_map/temporal_loops/pallas_call | solution.py:309
  48.8 1.3 %copy.6 = f32[2,3,3,1,2,128]{5,4,3,2,1,0:T(2,128)} copy(f32[2,3,3,1,2,128]{5,4,3,2,1,0:T(2,128)} %bitcast.10) | data formatting | bytes 36864

commit v2 on v1

v2 whole, which is shorter than its diff:
```python
import jax
import jax.numpy as jnp
from jax import lax
from jax.experimental import pallas as pl
from jax.experimental.pallas import tpu as pltpu
from jax.sharding import PartitionSpec as P

LX = 8
LY = 16
LANES = LX * LY
MESH = pl.DeviceIdType.MESH


def factors(count):
    first = 4 if count % 4 == 0 and count > 8 else 2
    rest = count // first
    third = 4 if rest % 4 == 0 and rest > 4 else 2
    return first, rest // third, third


def entry(matrix, row, col, adjoint):
    if adjoint:
        return matrix[col * 3 + row], matrix[9 + col * 3 + row], -1
    return matrix[row * 3 + col], matrix[9 + row * 3 + col], 1


def tile_product(left, right, left_adjoint=False, right_adjoint=False):
    real, imag = [], []
    for row in range(3):
        for col in range(3):
            re = im = None
            for mid in range(3):
                a, b, s = entry(left, row, mid, left_adjoint)
                c, d, r = entry(right, mid, col, right_adjoint)
                ac, bd, ad, bc = a * c, b * d, a * d, b * c
                re_term = ac - bd if s * r > 0 else ac + bd
                re = re_term if re is None else re + re_term
                if im is None:
                    if r > 0:
                        im = ad + bc if s > 0 else ad - bc
                    else:
                        im = bc - ad if s > 0 else -(ad + bc)
                else:
                    im = im + ad if r > 0 else im - ad
                    im = im + bc if s > 0 else im - bc
            real.append(re)
            imag.append(im)
    return real + imag


def tile_helpers():
    group = lax.broadcasted_iota(jnp.int32, (8, LANES), 0) // 2
    y = lax.broadcasted_iota(jnp.int32, (8, LANES), 1) % LY

    def pick(tiles):
        rest = jnp.where(group == 2, tiles[2], tiles[3])
        return jnp.where(group == 0, tiles[0], jnp.where(group == 1, tiles[1], rest))

    def x_plus(tile):
        return pltpu.roll(tile, LANES - LY, 1)

    def x_minus(tile):
        return pltpu.roll(tile, LY, 1)

    def y_plus(tile):
        return jnp.where(
            y == LY - 1, pltpu.roll(tile, LY - 1, 1), pltpu.roll(tile, LANES - 1, 1)
        )

    def y_minus(tile):
        return jnp.where(
            y == 0, pltpu.roll(tile, LANES - LY + 1, 1), pltpu.roll(tile, 1, 1)
        )

    return group, pick, x_plus, x_minus, y_plus, y_minus


def plus_unity(matrix):
    return [v + 1.0 if i in (0, 4, 8) else v for i, v in enumerate(matrix)]


def flowed_link(link, total):
    omega = tile_product(link, total)
    trace = (omega[9] + omega[13] + omega[17]) * (1.0 / 3.0)
    generator = [None] * 18
    for row in range(3):
        for col in range(3):
            a, b = row * 3 + col, col * 3 + row
            generator[a] = -0.125 * (omega[a] - omega[b])
            part = 0.5 * (omega[9 + a] + omega[9 + b])
            if row == col:
                part = part - trace
            generator[9 + a] = -0.25 * part
    series = plus_unity([v * (1.0 / 6.0) for v in generator])
    for order in range(5, 0, -1):
        series = tile_product(generator, series)
        series = plus_unity([v * (1.0 / order) for v in series])
    return tile_product(series, link)


def both_staples(a, b, c, d, e, f):
    upper = tile_product(tile_product(a, b, False, True), c, False, True)
    lower = tile_product(tile_product(d, e, True, True), f)
    return [v + w for v, w in zip(upper, lower)]


def pack_own(u, pk):
    for i in range(18):
        for mu in range(4):
            pk[0, i, 2 * mu : 2 * mu + 2, :] = u[mu, i]


def flow_line(u, tp, cz, zm0, zm3, zp0, pk, sides, line):
    group, pick, x_plus, x_minus, y_plus, y_minus = tile_helpers()
    for i in range(18):
        for mu in range(1, 4):
            pk[1, i, 2 * mu : 2 * mu + 2, :] = tp[mu - 1, i]
        sides[0, i, 6:7, :] = u[0, i, 1:2]
        sides[0, i, 7:8, :] = zp0[0, i]
        sides[1, i, 6:7, :] = cz[0, i, 1:2]
        sides[1, i, 7:8, :] = tp[2, i, 0:1]
        sides[2, i, 6:7, :] = zm0[0, i]
        sides[2, i, 7:8, :] = u[0, i, 0:1]
        sides[3, i, 6:7, :] = zm3[0, i]
        sides[3, i, 7:8, :] = u[3, i, 0:1]
    first = group == 0

    def spread(tile):
        tile = tile + pltpu.roll(tile, 4, 0)
        return tile + pltpu.roll(tile, 2, 0)

    here = [pk[0, i] for i in range(18)]
    ahead = [pk[1, i] for i in range(18)]
    link = [spread(jnp.where(first, tile, 0.0)) for tile in here]
    side = [[sides[f, i] for i in range(18)] for f in range(4)]
    b = [pick([v, x_plus(v), y_plus(v), s]) for v, s in zip(link, side[0])]
    d = [pick([v, x_minus(v), y_minus(v), s]) for v, s in zip(ahead, side[1])]
    e = [pick([v, x_minus(v), y_minus(v), s]) for v, s in zip(link, side[2])]
    f = [pick([v, x_minus(v), y_minus(v), s]) for v, s in zip(here, side[3])]
    total = both_staples(ahead, b, here, d, e, f)
    total = [spread(jnp.where(first, 0.0, v)) for v in total]
    result = flowed_link(link, total)
    for i in range(18):
        line[i // 9, (i // 3) % 3, i % 3] = result[i][0:2]


def flow_all(u, tp, tm, cz, ct, zm0, zm12, zm3, zp0, zp12, pk, fields, result):
    group, pick, x_plus, x_minus, y_plus, y_minus = tile_helpers()
    for i in range(18):
        below = (zm0[0, i], zm12[0, i], zm12[1, i], zm3[0, i])
        above = (zp0[0, i], zp12[0, i], zp12[1, i])
        for mu in range(4):
            pk[2, i, 2 * mu : 2 * mu + 2, :] = tm[mu, i]
            pk[4, i, 2 * mu : 2 * mu + 1, :] = below[mu]
            pk[4, i, 2 * mu + 1 : 2 * mu + 2, :] = u[mu, i, 0:1]
            if mu < 3:
                pk[3, i, 2 * mu : 2 * mu + 1, :] = u[mu, i, 1:2]
                pk[3, i, 2 * mu + 1 : 2 * mu + 2, :] = above[mu]
        pk[5, i, 0:1, :] = tm[0, i, 1:2]
        pk[5, i, 1:2, :] = ct[0, i, 0:1]
        pk[5, i, 6:7, :] = cz[0, i, 1:2]
        pk[5, i, 7:8, :] = tp[2, i, 0:1]

    def lowered(tile, k):
        return pltpu.roll(tile, 8 - 2 * k, 0)

    def pack_fields(i):
        here, t_up, t_down, z_up, z_down, corner = (pk[f, i] for f in range(6))
        up = [t_up, x_plus(here), y_plus(here), z_up]
        down = [t_down, x_minus(here), y_minus(here), z_down]
        base = pick(down)
        t_side = [None, corner, y_plus(t_down), x_plus(t_down)]
        z_side = [None, y_plus(z_down), x_plus(z_down), corner]
        for k in range(1, 4):
            ahead = pick([up[(nu - k) % 4] for nu in range(4)])
            behind = pick([down[(nu - k) % 4] for nu in range(4)])
            cross = pick([t_side[k], x_minus(ahead), y_minus(ahead), z_side[k]])
            fields[0, k - 1, i] = lowered(ahead, k)
            fields[1, 3 - k, i] = ahead
            fields[2, k - 1, i] = lowered(here, k)
            fields[3, k - 1, i] = lowered(cross, k)
            fields[4, 3 - k, i] = behind
            fields[5, k - 1, i] = lowered(base, k)

    for i in range(18):
        pack_fields(i)
    total = None
    for k in range(3):
        mats = [[fields[field, k, i] for i in range(18)] for field in range(6)]
        both = both_staples(*mats)
        total = both if total is None else [a + b for a, b in zip(total, both)]
    flowed = flowed_link([pk[0, i] for i in range(18)], total)
    for i in range(18):
        result[i] = flowed[i]


def product(left, right):
    re = im = None
    for mid in range(3):
        a, b = left[0][:, mid : mid + 1], left[1][:, mid : mid + 1]
        c, d = right[0][mid : mid + 1], right[1][mid : mid + 1]
        re_term, im_term = a * c - b * d, a * d + b * c
        re = re_term if re is None else re + re_term
        im = im_term if im is None else im + im_term
    return re, im


def sweep_kernel(count_t, count_z, links, result, out, u, tp, tm, cz, ct, zm0, zm12, zm3, zp0, zp12,
                 pk, sides, fields, line, slots1, slots2, slots3, row_total, plane_total,
                 own_sem, halo_send, halo_recv, send, recv):
    t = lax.axis_index("ta")
    z = lax.axis_index("gz")
    t_next, t_prev = lax.rem(t + 1, count_t), lax.rem(t + count_t - 1, count_t)
    z_next, z_prev = lax.rem(z + 1, count_z), lax.rem(z + count_z - 1, count_z)
    sizes = factors(count_t)
    strides = (1, sizes[0], sizes[0] * sizes[1])
    digits = [lax.rem(t // stride, size) for stride, size in zip(strides, sizes)]
    slots = (slots1, slots2, slots3)

    def peer(stage, offset):
        size, stride, digit = sizes[stage], strides[stage], digits[stage]
        moved = lax.rem(digit + size - offset, size)
        return (t + (moved - digit) * stride, z)

    halo_peers = [
        (t_prev, z), (t_next, z), (t, z_next), (t, z_prev), (t_prev, z_next), (t_next, z_prev)
    ]
    peers = halo_peers + [peer(s, d) for s in range(3) for d in range(1, sizes[s])]
    barrier = pltpu.get_barrier_semaphore()
    for other in peers:
        pl.semaphore_signal(barrier, inc=1, device_id=other, device_id_type=MESH)
    own = pltpu.make_async_copy(links, u, own_sem)
    own.start()
    own.wait()
    pack_own(u, pk)
    pl.semaphore_wait(barrier, len(peers))

    def layer(first, size, row):
        return u.at[pl.ds(first, size), :, pl.ds(row, 1), :]

    plan = [
        (u.at[pl.ds(3, 1)], cz, (t_prev, z_next)),
        (layer(0, 1, 1), zm0, (t, z_next)),
        (layer(3, 1, 1), zm3, (t, z_next)),
        (layer(0, 1, 0), zp0, (t, z_prev)),
        (u.at[pl.ds(1, 3)], tp, (t_prev, z)),
        (u.at[pl.ds(0, 1)], ct, (t_next, z_prev)),
        (u, tm, (t_next, z)),
        (layer(1, 2, 1), zm12, (t, z_next)),
        (layer(1, 2, 0), zp12, (t, z_prev)),
    ]
    halos = [
        pltpu.make_async_remote_copy(
            src_ref=source,
            dst_ref=target,
            send_sem=halo_send.at[index],
            recv_sem=halo_recv.at[index],
            device_id=other,
            device_id_type=MESH,
        )
        for index, (source, target, other) in enumerate(plan)
    ]
    for copy in halos[:7]:
        copy.start()
    for copy in halos[:5]:
        copy.wait_recv()
    for copy in halos[7:]:
        copy.start()
    flow_line(u, tp, cz, zm0, zm3, zp0, pk, sides, line)

    shape = (3, 3) + line.shape[-2:]
    diagonal = [
        [jnp.full(shape[2:], 1.0 if a == b else 0.0, jnp.float32) for b in range(3)]
        for a in range(3)
    ]
    unity = jnp.stack([jnp.stack(row) for row in diagonal])
    nought = jnp.zeros(shape, jnp.float32)
    start = [0, sizes[0] - 1, sizes[0] + sizes[1] - 2]

    def share(stage, source):
        copies = []
        for offset in range(1, sizes[stage]):
            index = start[stage] + offset - 1
            copies.append(
                pltpu.make_async_remote_copy(
                    src_ref=source,
                    dst_ref=slots[stage].at[offset - 1],
                    send_sem=send.at[index],
                    recv_sem=recv.at[index],
                    device_id=peer(stage, offset),
                    device_id_type=MESH,
                )
            )
        for copy in copies:
            copy.start()
        return copies

    def ordered(stage, copies):
        after = before = None
        for offset in range(1, sizes[stage]):
            copies[offset - 1].wait_recv()
            re, im = slots[stage][offset - 1, 0], slots[stage][offset - 1, 1]
            inside = digits[stage] + offset < sizes[stage]
            high = (jnp.where(inside, re, unity), jnp.where(inside, im, nought))
            low = (jnp.where(inside, unity, re), jnp.where(inside, nought, im))
            after = high if after is None else product(after, high)
            before = low if before is None else product(before, low)
        return after, before

    copies1 = share(0, line)
    row_after, row_before = ordered(0, copies1)
    row_after = product((line[0], line[1]), row_after)
    row = product(row_before, row_after)
    row_total[0], row_total[1] = row
    copies2 = share(1, row_total)
    for copy in halos[5:]:
        copy.wait_recv()
    flow_all(u, tp, tm, cz, ct, zm0, zm12, zm3, zp0, zp12, pk, fields, result)
    plane_after, plane_before = ordered(1, copies2)
    plane = product(plane_before, product(row, plane_after))
    plane_total[0], plane_total[1] = plane
    copies3 = share(2, plane_total)
    left = product(row_after, plane_after)
    right = product(plane_before, row_before)
    for offset in range(1, sizes[2]):
        copies3[offset - 1].wait_recv()
        left = product(left, (slots3[offset - 1, 0], slots3[offset - 1, 1]))
    out[0], out[1] = product(left, right)
    for copy in halos + copies1 + copies2 + copies3:
        copy.wait_send()


def sweep(links, count_t, count_z):
    sizes = factors(count_t)
    messages = sum(sizes) - 3
    matrix = (2, 3, 3, 2, LANES)

    def space(*shape):
        return pltpu.VMEM(shape, jnp.float32)

    vmem = pl.BlockSpec(memory_space=pltpu.VMEM)
    return pl.pallas_call(
        lambda *refs: sweep_kernel(count_t, count_z, *refs),
        out_shape=[
            jax.ShapeDtypeStruct((18, 8, LANES), jnp.float32),
            jax.ShapeDtypeStruct(matrix, jnp.float32),
        ],
        in_specs=[pl.BlockSpec(memory_space=pl.ANY)],
        out_specs=[vmem] * 2,
        scratch_shapes=[
            space(4, 18, 2, LANES),
            space(3, 18, 2, LANES),
            space(4, 18, 2, LANES),
            space(1, 18, 2, LANES),
            space(1, 18, 2, LANES),
            space(1, 18, 1, LANES),
            space(2, 18, 1, LANES),
            space(1, 18, 1, LANES),
            space(1, 18, 1, LANES),
            space(2, 18, 1, LANES),
            space(6, 18, 8, LANES),
            space(4, 18, 8, LANES),
            space(6, 3, 18, 8, LANES),
            space(*matrix),
            space(sizes[0] - 1, *matrix),
            space(sizes[1] - 1, *matrix),
            space(sizes[2] - 1, *matrix),
            space(*matrix),
            space(*matrix),
            pltpu.SemaphoreType.DMA,
            pltpu.SemaphoreType.DMA((9,)),
            pltpu.SemaphoreType.DMA((9,)),
            pltpu.SemaphoreType.DMA((messages,)),
            pltpu.SemaphoreType.DMA((messages,)),
        ],
        compiler_params=pltpu.CompilerParams(collective_id=0, has_side_effects=True),
        name="halo_flow_loops",
    )(links)


def unpack_kernel(packed, product_in, flowed, loops):
    for i in range(18):
        for mu in range(4):
            flowed[mu, i] = packed[i, 2 * mu : 2 * mu + 2, :]
    loops[...] = product_in[...]


def unpacked(packed, loops):
    vmem = pl.BlockSpec(memory_space=pltpu.VMEM)
    return pl.pallas_call(
        unpack_kernel,
        out_shape=[
            jax.ShapeDtypeStruct((4, 18, 2, LANES), jnp.float32),
            jax.ShapeDtypeStruct(loops.shape, jnp.float32),
        ],
        in_specs=[vmem] * 2,
        out_specs=[vmem] * 2,
        name="unpack",
    )(packed, loops)


def local(links):
    count_t, count_z = lax.axis_size("ta"), lax.axis_size("gz")
    packed, loops = sweep(links.reshape(4, 18, 2, LANES), count_t, count_z)
    flowed, loops = unpacked(packed, loops)
    return flowed.reshape(links.shape), loops.reshape(2, 3, 3, 1, 2, LANES)


def solution(mesh):
    return jax.shard_map(
        local,
        mesh=mesh,
        in_specs=(P(None, None, None, None, "ta", "gz", None),),
        out_specs=(
            P(None, None, None, None, "ta", "gz", None),
            P(None, None, None, "ta", "gz", None),
        ),
        check_vma=False,
    )
```

time: 50.5 us -> 42.1 us (0.83)
  the two profiles are of different devices: /device:TPU:2 before, /device:TPU:24 now
where the time goes in v2:
time: 42.1 us; the launch traced here: 41.9 us
  Pallas kernels  41.3 us (98%)
  between operations  0.64 us (2%)
    pallas_call x1, Pallas kernels, sweep(): pl.pallas_call(lambda *refs: sweep_kernel(count_t, count_z, *refs), out_s...  39.7 us
    pallas_call x1, Pallas kernels, unpacked(): pl.pallas_call(unpack_kernel, out_shape=[jax.ShapeDtypeStruct((4, 18, 2,...  1.55 us

profile of v2, /device:TPU:24, one launch (start us, length us, event | category | flops | bytes accessed | tf_op | source)
XLA Modules:
  0.0 41.9 jit_solution(17144108570624257785)
XLA Ops:
  0.6 39.7 %halo_flow_loops.1 = (f32[18,8,128]{2,1,0:T(8,128)}, f32[2,3,3,2,128]{4,3,2,1,0:T(2,128)}) custom-call(f32[4,18,2,128]{3,2,1,0:T(2,128)} %bitcast.7), custom_call_target="tpu_custom_call" | custom-call | tf_op jit(solution)/shard_map/halo_flow_loops/pallas_call | solution.py:342
  40.4 1.5 %unpack.1 = (f32[4,18,2,128]{3,2,1,0:T(2,128)}, f32[2,3,3,2,128]{4,3,2,1,0:T(2,128)}) custom-call(f32[18,8,128]{2,1,0:T(8,128)} %get-tuple-element.6.packed, f32[2,3,3,2,128]{4,3,2,1,0:T(2,128)} %get-tuple-element.7.product_in), custom_call_target="tpu_custom_call" | custom-call | tf_op jit(solution)/shard_map/unpack/pallas_call | solution.py:390

commit v3 on v2

--- a/solution.py
+++ b/solution.py
@@ -231,21 +231,19 @@
         pl.semaphore_signal(barrier, inc=1, device_id=other, device_id_type=MESH)
     own = pltpu.make_async_copy(links, u, own_sem)
     own.start()
-    own.wait()
-    pack_own(u, pk)
     pl.semaphore_wait(barrier, len(peers))
 
     def layer(first, size, row):
-        return u.at[pl.ds(first, size), :, pl.ds(row, 1), :]
+        return links.at[pl.ds(first, size), :, pl.ds(row, 1), :]
 
     plan = [
-        (u.at[pl.ds(3, 1)], cz, (t_prev, z_next)),
+        (links.at[pl.ds(3, 1)], cz, (t_prev, z_next)),
         (layer(0, 1, 1), zm0, (t, z_next)),
         (layer(3, 1, 1), zm3, (t, z_next)),
         (layer(0, 1, 0), zp0, (t, z_prev)),
-        (u.at[pl.ds(1, 3)], tp, (t_prev, z)),
-        (u.at[pl.ds(0, 1)], ct, (t_next, z_prev)),
-        (u, tm, (t_next, z)),
+        (links.at[pl.ds(1, 3)], tp, (t_prev, z)),
+        (links.at[pl.ds(0, 1)], ct, (t_next, z_prev)),
+        (links, tm, (t_next, z)),
         (layer(1, 2, 1), zm12, (t, z_next)),
         (layer(1, 2, 0), zp12, (t, z_prev)),
     ]
@@ -262,6 +260,8 @@
     ]
     for copy in halos[:7]:
         copy.start()
+    own.wait()
+    pack_own(u, pk)
     for copy in halos[:5]:
         copy.wait_recv()
     for copy in halos[7:]:
@@ -313,15 +313,15 @@
     row = product(row_before, row_after)
     row_total[0], row_total[1] = row
     copies2 = share(1, row_total)
-    for copy in halos[5:]:
-        copy.wait_recv()
-    flow_all(u, tp, tm, cz, ct, zm0, zm12, zm3, zp0, zp12, pk, fields, result)
     plane_after, plane_before = ordered(1, copies2)
     plane = product(plane_before, product(row, plane_after))
     plane_total[0], plane_total[1] = plane
     copies3 = share(2, plane_total)
     left = product(row_after, plane_after)
     right = product(plane_before, row_before)
+    for copy in halos[5:]:
+        copy.wait_recv()
+    flow_all(u, tp, tm, cz, ct, zm0, zm12, zm3, zp0, zp12, pk, fields, result)
     for offset in range(1, sizes[2]):
         copies3[offset - 1].wait_recv()
         left = product(left, (slots3[offset - 1, 0], slots3[offset - 1, 1]))

time: 42.1 us -> 42.3 us (level)
  no operation moved by 1% of the time
where the time goes in v3:
time: 42.3 us; the launch traced here: 42.1 us
  Pallas kernels  41.5 us (98%)
  between operations  0.64 us (2%)
    pallas_call x1, Pallas kernels, sweep(): pl.pallas_call(lambda *refs: sweep_kernel(count_t, count_z, *refs), out_s...  40 us
    pallas_call x1, Pallas kernels, unpacked(): pl.pallas_call(unpack_kernel, out_shape=[jax.ShapeDtypeStruct((4, 18, 2,...  1.55 us

profile of v3, /device:TPU:24, one launch (start us, length us, event | category | flops | bytes accessed | tf_op | source)
XLA Modules:
  0.0 42.1 jit_solution(15393456198471493790)
XLA Ops:
  0.6 40.0 %halo_flow_loops.1 = (f32[18,8,128]{2,1,0:T(8,128)}, f32[2,3,3,2,128]{4,3,2,1,0:T(2,128)}) custom-call(f32[4,18,2,128]{3,2,1,0:T(2,128)} %bitcast.7), custom_call_target="tpu_custom_call" | custom-call | tf_op jit(solution)/shard_map/halo_flow_loops/pallas_call | solution.py:342
  40.6 1.5 %unpack.1 = (f32[4,18,2,128]{3,2,1,0:T(2,128)}, f32[2,3,3,2,128]{4,3,2,1,0:T(2,128)}) custom-call(f32[18,8,128]{2,1,0:T(8,128)} %get-tuple-element.6.packed, f32[2,3,3,2,128]{4,3,2,1,0:T(2,128)} %get-tuple-element.7.product_in), custom_call_target="tpu_custom_call" | custom-call | tf_op jit(solution)/shard_map/unpack/pallas_call | solution.py:390

commit v4 on v3

--- a/solution.py
+++ b/solution.py
@@ -117,7 +117,7 @@
             pk[1, i, 2 * mu : 2 * mu + 2, :] = tp[mu - 1, i]
         sides[0, i, 6:7, :] = u[0, i, 1:2]
         sides[0, i, 7:8, :] = zp0[0, i]
-        sides[1, i, 6:7, :] = cz[0, i, 1:2]
+        sides[1, i, 6:7, :] = cz[0, i]
         sides[1, i, 7:8, :] = tp[2, i, 0:1]
         sides[2, i, 6:7, :] = zm0[0, i]
         sides[2, i, 7:8, :] = u[0, i, 0:1]
@@ -157,8 +157,8 @@
                 pk[3, i, 2 * mu : 2 * mu + 1, :] = u[mu, i, 1:2]
                 pk[3, i, 2 * mu + 1 : 2 * mu + 2, :] = above[mu]
         pk[5, i, 0:1, :] = tm[0, i, 1:2]
-        pk[5, i, 1:2, :] = ct[0, i, 0:1]
-        pk[5, i, 6:7, :] = cz[0, i, 1:2]
+        pk[5, i, 1:2, :] = ct[0, i]
+        pk[5, i, 6:7, :] = cz[0, i]
         pk[5, i, 7:8, :] = tp[2, i, 0:1]
 
     def lowered(tile, k):
@@ -237,12 +237,12 @@
         return links.at[pl.ds(first, size), :, pl.ds(row, 1), :]
 
     plan = [
-        (links.at[pl.ds(3, 1)], cz, (t_prev, z_next)),
+        (layer(3, 1, 1), cz, (t_prev, z_next)),
         (layer(0, 1, 1), zm0, (t, z_next)),
         (layer(3, 1, 1), zm3, (t, z_next)),
         (layer(0, 1, 0), zp0, (t, z_prev)),
         (links.at[pl.ds(1, 3)], tp, (t_prev, z)),
-        (links.at[pl.ds(0, 1)], ct, (t_next, z_prev)),
+        (layer(0, 1, 0), ct, (t_next, z_prev)),
         (links, tm, (t_next, z)),
         (layer(1, 2, 1), zm12, (t, z_next)),
         (layer(1, 2, 0), zp12, (t, z_prev)),
@@ -291,8 +291,9 @@
                     device_id_type=MESH,
                 )
             )
-        for copy in copies:
-            copy.start()
+        size = sizes[stage]
+        for offset in sorted(range(1, size), key=lambda d: -min(d, size - d)):
+            copies[offset - 1].start()
         return copies
 
     def ordered(stage, copies):
@@ -341,18 +342,15 @@
     vmem = pl.BlockSpec(memory_space=pltpu.VMEM)
     return pl.pallas_call(
         lambda *refs: sweep_kernel(count_t, count_z, *refs),
-        out_shape=[
-            jax.ShapeDtypeStruct((18, 8, LANES), jnp.float32),
-            jax.ShapeDtypeStruct(matrix, jnp.float32),
-        ],
+        out_shape=[space(18, 8, LANES), space(*matrix)],
         in_specs=[pl.BlockSpec(memory_space=pl.ANY)],
         out_specs=[vmem] * 2,
         scratch_shapes=[
             space(4, 18, 2, LANES),
             space(3, 18, 2, LANES),
             space(4, 18, 2, LANES),
-            space(1, 18, 2, LANES),
-            space(1, 18, 2, LANES),
+            space(1, 18, 1, LANES),
+            space(1, 18, 1, LANES),
             space(1, 18, 1, LANES),
             space(2, 18, 1, LANES),
             space(1, 18, 1, LANES),
@@ -396,7 +394,7 @@
         in_specs=[vmem] * 2,
         out_specs=[vmem] * 2,
         name="unpack",
-    )(packed, loops)
+    )(*(pltpu.with_memory_space_constraint(v, pltpu.VMEM) for v in (packed, loops)))
 
 
 def local(links):

time: 42.3 us -> 39.5 us (0.934)
  the two profiles are of different devices: /device:TPU:24 before, /device:TPU:8 now
where the time goes in v4:
time: 39.5 us; the launch traced here: 39.4 us
  Pallas kernels  38.7 us (98%)
  between operations  0.64 us (2%)
    pallas_call x1, Pallas kernels, sweep(): pl.pallas_call(lambda *refs: sweep_kernel(count_t, count_z, *refs), out_s...  38.1 us

profile of v4, /device:TPU:8, one launch (start us, length us, event | category | flops | bytes accessed | tf_op | source)
XLA Modules:
  0.0 39.4 jit_solution(13443161658670783039)
XLA Ops:
  0.6 38.1 %halo_flow_loops.1 = (f32[18,8,128]{2,1,0:T(8,128)S(1)}, f32[2,3,3,2,128]{4,3,2,1,0:T(2,128)S(1)}) custom-call(f32[4,18,2,128]{3,2,1,0:T(2,128)} %bitcast.7), custom_call_target="tpu_custom_call" | custom-call | tf_op jit(solution)/shard_map/halo_flow_loops/pallas_call | solution.py:343
  38.7 0.7 %unpack.1 = (f32[4,18,2,128]{3,2,1,0:T(2,128)}, f32[2,3,3,2,128]{4,3,2,1,0:T(2,128)}) custom-call(f32[18,8,128]{2,1,0:T(8,128)S(1)} %get-tuple-element.6.packed, f32[2,3,3,2,128]{4,3,2,1,0:T(2,128)S(1)} %get-tuple-element.7.product_in), custom_call_target="tpu_custom_call" | custom-call | tf_op jit(solution)/shard_map/unpack/pallas_call | solution.py:388

commit v5 on v4

--- a/solution.py
+++ b/solution.py
@@ -110,9 +110,21 @@
             pk[0, i, 2 * mu : 2 * mu + 2, :] = u[mu, i]
 
 
+KEPT = tuple(range(6)) + tuple(range(9, 15))
+
+
+def restore_row(tiles):
+    for col in range(3):
+        k, m = (col + 1) % 3, (col + 2) % 3
+        ak, am, bk, bm = tiles[k], tiles[m], tiles[3 + k], tiles[3 + m]
+        ck, cm, dk, dm = tiles[9 + k], tiles[9 + m], tiles[12 + k], tiles[12 + m]
+        tiles[6 + col] = (ak * bm - ck * dm) - (am * bk - cm * dk)
+        tiles[15 + col] = (am * dk + cm * bk) - (ak * dm + ck * bm)
+
+
 def flow_line(u, tp, cz, zm0, zm3, zp0, pk, sides, line):
     group, pick, x_plus, x_minus, y_plus, y_minus = tile_helpers()
-    for i in range(18):
+    for i in KEPT:
         for mu in range(1, 4):
             pk[1, i, 2 * mu : 2 * mu + 2, :] = tp[mu - 1, i]
         sides[0, i, 6:7, :] = u[0, i, 1:2]
@@ -123,6 +135,9 @@
         sides[2, i, 7:8, :] = u[0, i, 0:1]
         sides[3, i, 6:7, :] = zm3[0, i]
         sides[3, i, 7:8, :] = u[3, i, 0:1]
+    restore_row(pk.at[1])
+    for f in range(4):
+        restore_row(sides.at[f])
     first = group == 0
 
     def spread(tile):
@@ -144,11 +159,11 @@
         line[i // 9, (i // 3) % 3, i % 3] = result[i][0:2]
 
 
-def flow_all(u, tp, tm, cz, ct, zm0, zm12, zm3, zp0, zp12, pk, fields, result):
+def flow_all(u, tm, ct, zm12, zp12, pk, sides, fields, result):
     group, pick, x_plus, x_minus, y_plus, y_minus = tile_helpers()
     for i in range(18):
-        below = (zm0[0, i], zm12[0, i], zm12[1, i], zm3[0, i])
-        above = (zp0[0, i], zp12[0, i], zp12[1, i])
+        below = (sides[2, i, 6:7], zm12[0, i], zm12[1, i], sides[3, i, 6:7])
+        above = (sides[0, i, 7:8], zp12[0, i], zp12[1, i])
         for mu in range(4):
             pk[2, i, 2 * mu : 2 * mu + 2, :] = tm[mu, i]
             pk[4, i, 2 * mu : 2 * mu + 1, :] = below[mu]
@@ -158,8 +173,7 @@
                 pk[3, i, 2 * mu + 1 : 2 * mu + 2, :] = above[mu]
         pk[5, i, 0:1, :] = tm[0, i, 1:2]
         pk[5, i, 1:2, :] = ct[0, i]
-        pk[5, i, 6:7, :] = cz[0, i]
-        pk[5, i, 7:8, :] = tp[2, i, 0:1]
+        pk[5, i, 6:8, :] = sides[1, i, 6:8]
 
     def lowered(tile, k):
         return pltpu.roll(tile, 8 - 2 * k, 0)
@@ -233,15 +247,23 @@
     own.start()
     pl.semaphore_wait(barrier, len(peers))
 
+    def two_rows(source, target, other):
+        return [
+            (source.at[:, pl.ds(first, 6)], target.at[:, pl.ds(first, 6)], other)
+            for first in (0, 9)
+        ]
+
     def layer(first, size, row):
         return links.at[pl.ds(first, size), :, pl.ds(row, 1), :]
 
-    plan = [
+    critical = [
         (layer(3, 1, 1), cz, (t_prev, z_next)),
         (layer(0, 1, 1), zm0, (t, z_next)),
         (layer(3, 1, 1), zm3, (t, z_next)),
         (layer(0, 1, 0), zp0, (t, z_prev)),
         (links.at[pl.ds(1, 3)], tp, (t_prev, z)),
+    ]
+    plan = [item for whole in critical for item in two_rows(*whole)] + [
         (layer(0, 1, 0), ct, (t_next, z_prev)),
         (links, tm, (t_next, z)),
         (layer(1, 2, 1), zm12, (t, z_next)),
@@ -258,13 +280,13 @@
         )
         for index, (source, target, other) in enumerate(plan)
     ]
-    for copy in halos[:7]:
+    for copy in halos[:12]:
         copy.start()
     own.wait()
     pack_own(u, pk)
-    for copy in halos[:5]:
+    for copy in halos[:10]:
         copy.wait_recv()
-    for copy in halos[7:]:
+    for copy in halos[12:]:
         copy.start()
     flow_line(u, tp, cz, zm0, zm3, zp0, pk, sides, line)
 
@@ -320,9 +342,9 @@
     copies3 = share(2, plane_total)
     left = product(row_after, plane_after)
     right = product(plane_before, row_before)
-    for copy in halos[5:]:
+    for copy in halos[10:]:
         copy.wait_recv()
-    flow_all(u, tp, tm, cz, ct, zm0, zm12, zm3, zp0, zp12, pk, fields, result)
+    flow_all(u, tm, ct, zm12, zp12, pk, sides, fields, result)
     for offset in range(1, sizes[2]):
         copies3[offset - 1].wait_recv()
         left = product(left, (slots3[offset - 1, 0], slots3[offset - 1, 1]))
@@ -366,8 +388,8 @@
             space(*matrix),
             space(*matrix),
             pltpu.SemaphoreType.DMA,
-            pltpu.SemaphoreType.DMA((9,)),
-            pltpu.SemaphoreType.DMA((9,)),
+            pltpu.SemaphoreType.DMA((14,)),
+            pltpu.SemaphoreType.DMA((14,)),
             pltpu.SemaphoreType.DMA((messages,)),
             pltpu.SemaphoreType.DMA((messages,)),
         ],

time: 39.5 us -> 39.7 us (level)
  no operation moved by 1% of the time
where the time goes in v5:
time: 39.7 us; the launch traced here: 39.6 us
  Pallas kernels  38.9 us (98%)
  between operations  0.64 us (2%)
    pallas_call x1, Pallas kernels, sweep(): pl.pallas_call(lambda *refs: sweep_kernel(count_t, count_z, *refs), out_s...  38.3 us

profile of v5, /device:TPU:8, one launch (start us, length us, event | category | flops | bytes accessed | tf_op | source)
XLA Modules:
  0.0 39.6 jit_solution(8851751909294878903)
XLA Ops:
  0.6 38.3 %halo_flow_loops.1 = (f32[18,8,128]{2,1,0:T(8,128)S(1)}, f32[2,3,3,2,128]{4,3,2,1,0:T(2,128)S(1)}) custom-call(f32[4,18,2,128]{3,2,1,0:T(2,128)} %bitcast.7), custom_call_target="tpu_custom_call" | custom-call | tf_op jit(solution)/shard_map/halo_flow_loops/pallas_call | solution.py:365
  38.9 0.7 %unpack.1 = (f32[4,18,2,128]{3,2,1,0:T(2,128)}, f32[2,3,3,2,128]{4,3,2,1,0:T(2,128)}) custom-call(f32[18,8,128]{2,1,0:T(8,128)S(1)} %get-tuple-element.6.packed, f32[2,3,3,2,128]{4,3,2,1,0:T(2,128)S(1)} %get-tuple-element.7.product_in), custom_call_target="tpu_custom_call" | custom-call | tf_op jit(solution)/shard_map/unpack/pallas_call | solution.py:410

commit v6 on v4

--- a/solution.py
+++ b/solution.py
@@ -268,13 +268,11 @@
         copy.start()
     flow_line(u, tp, cz, zm0, zm3, zp0, pk, sides, line)
 
-    shape = (3, 3) + line.shape[-2:]
     diagonal = [
-        [jnp.full(shape[2:], 1.0 if a == b else 0.0, jnp.float32) for b in range(3)]
+        [jnp.full((4, LANES), 1.0 if a == b else 0.0, jnp.float32) for b in range(3)]
         for a in range(3)
     ]
-    unity = jnp.stack([jnp.stack(row) for row in diagonal])
-    nought = jnp.zeros(shape, jnp.float32)
+    unity_rows = jnp.stack([jnp.stack(row) for row in diagonal])
     start = [0, sizes[0] - 1, sizes[0] + sizes[1] - 2]
 
     def share(stage, source):
@@ -297,15 +295,18 @@
         return copies
 
     def ordered(stage, copies):
-        after = before = None
+        both = None
+        rows = lax.broadcasted_iota(jnp.int32, (3, 3, 4, LANES), 2)
         for offset in range(1, sizes[stage]):
             copies[offset - 1].wait_recv()
-            re, im = slots[stage][offset - 1, 0], slots[stage][offset - 1, 1]
-            inside = digits[stage] + offset < sizes[stage]
-            high = (jnp.where(inside, re, unity), jnp.where(inside, im, nought))
-            low = (jnp.where(inside, unity, re), jnp.where(inside, nought, im))
-            after = high if after is None else product(after, high)
-            before = low if before is None else product(before, low)
+            inside = (digits[stage] + offset < sizes[stage]).astype(jnp.int32)
+            used = (rows // 2) + inside == 1
+            parts = [slots[stage][offset - 1, c] for c in range(2)]
+            re, im = (jnp.concatenate([part, part], axis=2) for part in parts)
+            factor = (jnp.where(used, re, unity_rows), jnp.where(used, im, 0.0))
+            both = factor if both is None else product(both, factor)
+        after = tuple(part[:, :, 0:2] for part in both)
+        before = tuple(part[:, :, 2:4] for part in both)
         return after, before
 
     copies1 = share(0, line)

time: 39.5 us -> 39.4 us (level)
  no operation moved by 1% of the time
where the time goes in v6:
time: 39.4 us; the launch traced here: 39.3 us
  Pallas kernels  38.7 us (98%)
  between operations  0.64 us (2%)
    pallas_call x1, Pallas kernels, sweep(): pl.pallas_call(lambda *refs: sweep_kernel(count_t, count_z, *refs), out_s...  38 us

profile of v6, /device:TPU:8, one launch (start us, length us, event | category | flops | bytes accessed | tf_op | source)
XLA Modules:
  0.0 39.3 jit_solution(18378899670989244807)
XLA Ops:
  0.6 38.0 %halo_flow_loops.1 = (f32[18,8,128]{2,1,0:T(8,128)S(1)}, f32[2,3,3,2,128]{4,3,2,1,0:T(2,128)S(1)}) custom-call(f32[4,18,2,128]{3,2,1,0:T(2,128)} %bitcast.7), custom_call_target="tpu_custom_call" | custom-call | tf_op jit(solution)/shard_map/halo_flow_loops/pallas_call | solution.py:344
  38.6 0.7 %unpack.1 = (f32[4,18,2,128]{3,2,1,0:T(2,128)}, f32[2,3,3,2,128]{4,3,2,1,0:T(2,128)}) custom-call(f32[18,8,128]{2,1,0:T(8,128)S(1)} %get-tuple-element.6.packed, f32[2,3,3,2,128]{4,3,2,1,0:T(2,128)S(1)} %get-tuple-element.7.product_in), custom_call_target="tpu_custom_call" | custom-call | tf_op jit(solution)/shard_map/unpack/pallas_call | solution.py:389
